TPU v7x, 32 devices: a whole 2x2x4 slice. The times are simulated.
32 devices in a mesh: row: 4 (over x, core), col: 8 (over z, y).
Axes of the slice: x: 2, y: 2, z: 4, core: 2. Of those that a mesh axis runs over, the one named last changes fastest.
Arguments:
- design: bfloat16 [18432, 2048], P(('row', 'col')), may hold values from -0.19921875 to 0.19921875
- arc_filter: bfloat16 [2048, 2048], replicated, may hold values from -0.59765625 to 0.59765625
- arc_of_row: int32 [2048], replicated, may hold values from 0 to 255, never falling along the last dimension, each value on 1 to 512 neighbouring positions
- terr_stored: bfloat16 [18432, 128], P(('row', 'col')), may hold values from -3 to 3
- block_order: int32 [144], P('row'), may hold values from 0 to 143, as said below
- directions: float32 [18432, 256], P(('row', 'col')), may hold values from -6 to 6
Outputs:
- normals: float32 [4, 8, 576, 18432], P(None, 'col', None, 'row')
- products: float32 [18432, 256], P(('row', 'col'))
Inputs may be any that keep to these rules, and one draw needn't show every extreme that they name: `arc_of_row`: arc numbers never fall along the observations. `block_order`: each aligned group of 36 consecutive entries (the blocks of one block of 4608 unknowns) is a permutation of the positions of that same group.
All inputs are finite; a program needn't handle non-finite values.
Results may differ from a plain program's by a relative error of at most 0.00045.
Values may be sent and summed in bfloat16 or wider, within the bound.
A program may use at most 192 MiB of HBM per device.

v0:
```python
import jax
import jax.numpy as jnp
from jax import lax
from jax.sharding import PartitionSpec as P


def whiten(design, arc_filter, arc_of_row):
    positions = jnp.arange(arc_filter.shape[0], dtype=jnp.int32)
    keep_mask = (positions[:, None] > positions[None, :]) & (
        arc_of_row[:, None] == arc_of_row[None, :]
    )
    lower_part = jnp.where(keep_mask, arc_filter, jnp.zeros_like(arc_filter))
    mixed_part = lax.dot_general(
        design, lower_part, (((1,), (1,)), ((), ())), preferred_element_type=jnp.float32
    )
    return (design.astype(jnp.float32) + mixed_part).astype(jnp.bfloat16)


def body(design, arc_filter, arc_of_row, terr_stored, block_order, directions):
    whitened = whiten(design, arc_filter, arc_of_row)
    own_width = whitened.shape[0]
    rows_block, terr_rows = (
        lax.all_gather(whitened, "col", axis=0, tiled=True),
        lax.all_gather(terr_stored, "col", axis=0, tiled=True),
    )
    cols_block = lax.all_gather(whitened, "row", axis=0, tiled=True)
    normal_tile = lax.dot_general(
        cols_block, rows_block, (((1,), (1,)), ((), ())), preferred_element_type=jnp.float32
    )
    block_size = terr_rows.shape[1]
    span_rows = terr_rows.shape[0]
    group_count = span_rows // block_size
    row_index = lax.axis_index("row")
    col_index = lax.axis_index("col")
    local_order = block_order - row_index * group_count
    selector = (local_order[None, :] == jnp.arange(group_count, dtype=jnp.int32)[:, None]).astype(
        jnp.float32
    )
    stored = terr_rows.astype(jnp.float32).reshape(group_count, block_size, block_size)
    symmetric = jnp.triu(stored) + jnp.swapaxes(jnp.triu(stored, 1), 1, 2)
    ordered = jnp.einsum(
        "qt,tab->qab", selector, symmetric, precision=lax.Precision.HIGHEST
    ).reshape(span_rows, block_size)
    own_rows = lax.dynamic_slice_in_dim(ordered, col_index * own_width, own_width, 0)
    positions = col_index * own_width + jnp.arange(own_width, dtype=jnp.int32)
    onehot = (
        (positions // block_size)[:, None] == jnp.arange(group_count, dtype=jnp.int32)[None, :]
    ).astype(jnp.float32)
    terr_added = (onehot[:, :, None] * own_rows[:, None, :]).reshape(own_width, span_rows)
    current = lax.dynamic_slice_in_dim(normal_tile, row_index * own_width, own_width, 0)
    normal_tile = lax.dynamic_update_slice_in_dim(
        normal_tile, current + terr_added, row_index * own_width, 0
    )
    tile_rows = normal_tile.shape[0]
    partial_sum = jnp.dot(
        normal_tile,
        lax.all_gather(directions, "col", axis=0, tiled=True),
        precision=lax.Precision.HIGHEST,
        preferred_element_type=jnp.float32,
    )
    products = lax.psum_scatter(partial_sum, "row", scatter_dimension=0, tiled=True)
    normals = normal_tile.reshape(tile_rows // own_width, 1, own_width, span_rows)
    return (normals, products)


def solution(mesh):
    return jax.shard_map(
        body,
        mesh=mesh,
        in_specs=(
            P(("row", "col"), None),
            P(),
            P(),
            P(("row", "col"), None),
            P("row"),
            P(("row", "col"), None),
        ),
        out_specs=(P(None, "col", None, "row"), P(("row", "col"), None)),
        check_vma=False,
    )
```

profile of v0, /device:TPU:0, one launch (start us, length us, event | category | flops | bytes accessed | tf_op | source)
XLA Modules:
  0.0 640.6 jit_solution(7251335784853604112)
XLA Ops:
  7.2 0.0 all-gather.9.cloned.1.call-start
  7.2 0.7 all-gather.9.cloned.1.call-update
  7.9 0.0 all-gather.5.cloned.1.call-start
  7.9 11.9 %fusion.7 = bf16[576,2048]{1,0:T(8,128)(2,1)} fusion(bf16[576,2048]{1,0:T(8,128)(2,1)} %param.6, bf16[2048,2048]{1,0:T(8,128)(2,1)} %param.7, s32[2048]{0:T(1024)} %param.8), kind=kOutput, calls=%fused_computation.10 | convolution fusion | flops 4852154368 | bytes 13115392 | tf_op jit(solution)/shard_map/dot_general | solution.py:13
  19.8 0.0 all-gather.7.cloned.1.call-start
  19.9 0.7 all-gather.7.cloned.1.call-update
  20.6 0.0 all-gather.11.cloned.1.call-start
  20.6 0.5 all-gather.11.cloned.1.call-update
  21.1 0.0 reduce-scatter.2.cloned.1.call-start
  21.3 0.1 fusion.15
  21.4 32.6 %all-gather.9.cloned.1.call-done = bf16[4608,128]{1,0:T(8,128)(2,1)} async-done(((bf16[576,128]{1,0:T(8,128)(2,1)}), bf16[4608,128]{1,0:T(8,128)(2,1)}) %all-gather.9.cloned.1.call-update) | async-done | bytes 1179664 | tf_op jit(solution)/shard_map/all_gather | solution.py:24
  54.0 1.9 copy.12
  56.0 1.8 broadcast_select_fusion
  57.8 3.4 copy.14
  61.2 3.8 fusion.11
  65.0 0.5 copy.15
  65.5 7.0 %broadcast_multiply_fusion = f32[576,36,128]{2,1,0:T(8,128)} fusion(f32[576,128]{1,0:T(8,128)S(1)} %constant_dynamic-slice_fusion, f32[576,36]{1,0:T(8,128)S(1)} %fusion.15), kind=kLoop, calls=%fused_computation.8 | loop fusion | flops 2654208 | bytes 10994688 | tf_op jit(solution)/shard_map/mul | solution.py:49
  72.5 46.0 %all-gather.5.cloned.1.call-done = bf16[2304,2048]{1,0:T(8,128)(2,1)} async-done(((bf16[576,2048]{1,0:T(8,128)(2,1)}), bf16[2304,2048]{1,0:T(8,128)(2,1)}) %all-gather.5.cloned.1.call-update) | async-done | bytes 9437200 | tf_op jit(solution)/shard_map/all_gather | solution.py:26
  118.5 364.0 %all-gather.7.cloned.1.call-done = bf16[4608,2048]{1,0:T(8,128)(2,1)} async-done(((bf16[576,2048]{1,0:T(8,128)(2,1)}), bf16[4608,2048]{1,0:T(8,128)(2,1)}) %all-gather.7.cloned.1.call-update) | async-done | bytes 18874384 | tf_op jit(solution)/shard_map/all_gather | solution.py:23
  482.5 53.3 %fusion.24 = f32[2304,4608]{1,0:T(8,128)} fusion(bf16[2304,2048]{1,0:T(8,128)(2,1)} %all-gather.5.cloned.1.call-done, bf16[4608,2048]{1,0:T(8,128)(2,1)} %all-gather.7.cloned.1.call-done), kind=kOutput, calls=%fused_computation.39 | convolution fusion | flops 43486543872 | bytes 70778880 | tf_op jit(solution)/shard_map/dot_general | solution.py:27
  535.8 10.3 %fusion.2 = f32[2304,4608]{1,0:T(8,128)} fusion(f32[2304,4608]{1,0:T(8,128)} %fusion.24, s32[]{:T(128)S(6)} %select_n.29, f32[72,8,36,128]{3,2,1,0:T(8,128)S(1)} %bitcast.27), kind=kLoop, calls=%fused_computation.4 | loop fusion | flops 2654208 | bytes 31850500 | tf_op jit(solution)/shard_map/dynamic_update_slice | solution.py:51
  546.1 17.8 %all-gather.11.cloned.1.call-done = f32[4608,256]{1,0:T(8,128)} async-done(((f32[576,256]{1,0:T(8,128)}), f32[4608,256]{1,0:T(8,128)}) %all-gather.11.cloned.1.call-update) | async-done | bytes 4718608 | tf_op jit(solution)/shard_map/all_gather | solution.py:57
  563.9 38.9 %fusion.25 = f32[2304,256]{1,0:T(8,128)} fusion(f32[2304,4608]{1,0:T(8,128)} %fusion.2, f32[4608,256]{1,0:T(8,128)} %all-gather.11.cloned.1.call-done), kind=kOutput, calls=%fused_computation.40 | convolution fusion | flops 32614907904 | bytes 49545216 | tf_op jit(solution)/shard_map/dot_general | solution.py:55
  602.8 31.3 %reduce-scatter.2.cloned.1.call-done = f32[576,256]{1,0:T(8,128)} async-done(((f32[2304,256]{1,0:T(8,128)}), f32[576,256]{1,0:T(8,128)}) %reduce-scatter.2.cloned.1.call-update) | async-done | bytes 589840 | tf_op jit(solution)/shard_map/reduce_scatter | solution.py:61
  (12 shorter events, 0.1 us)
Async XLA Ops:
  7.2 46.9 %all-gather.9.cloned.1.call-start = ((), (), s32[]{:S(2)}) async-start(), calls=%async_computation.3 | async-start | bytes 1327104 | tf_op jit(solution)/shard_map/all_gather | solution.py:24
  7.9 110.6 %all-gather.5.cloned.1.call-start = ((), (), s32[]{:S(2)}) async-start(), calls=%async_computation.1 | async-start | bytes 11796480 | tf_op jit(solution)/shard_map/all_gather | solution.py:26
  19.8 1.6 copy-start.1
  19.8 462.7 %all-gather.7.cloned.1.call-start = ((), (), s32[]{:S(2)}) async-start(), calls=%async_computation.2 | async-start | bytes 21233664 | tf_op jit(solution)/shard_map/all_gather | solution.py:23
  20.6 543.3 %all-gather.11.cloned.1.call-start = ((), (), s32[]{:S(2)}) async-start(), calls=%async_computation.4 | async-start | bytes 5308416 | tf_op jit(solution)/shard_map/all_gather | solution.py:57
  21.1 613.0 %reduce-scatter.2.cloned.1.call-start = ((), (), s32[]{:S(2)}) async-start(), calls=%async_computation.5 | async-start | bytes 2949120 | tf_op jit(solution)/shard_map/reduce_scatter | solution.py:61
  482.5 53.3 %copy-start = (f32[576,36,128]{2,1,0:T(8,128)S(1)}, f32[576,36,128]{2,1,0:T(8,128)}, u32[]{:S(2)}) copy-start(f32[576,36,128]{2,1,0:T(8,128)} %broadcast_multiply_fusion) | copy-start | bytes 31850500
Sparse Core Ops, SparseCore 0:
  10.2 43.8 all-gather.8
  55.6 62.8 all-gather.4
  120.1 362.3 all-gather.6
  484.5 79.2 all-gather.10
  602.9 31.1 reduce-scatter.1
where the time goes:
time: 641 us
  waiting for transfers between devices  494 us (77%)
  matrix products  108 us (17%)
  other arithmetic  19.3 us (3%)
  between operations  13.9 us (2%)
    all_gather x1, waiting for transfers between devices, body(): lax.all_gather(whitened, 'col', axis=0, tiled=True)  364 us
    dot_general x1, matrix products, body(): lax.dot_general(cols_block, rows_block, (((1,), (1,)), ((), ())), preferr...  53.3 us
    all_gather x1, waiting for transfers between devices, body(): cols_block = lax.all_gather(whitened, 'row', axis=0, tiled=True)  46 us
    dot_general x1, matrix products, body(): jnp.dot(normal_tile, lax.all_gather(directions, 'col', axis=0, tiled=True...  38.9 us
    all_gather x1, waiting for transfers between devices, body(): lax.all_gather(terr_stored, 'col', axis=0, tiled=True)  32.6 us
    reduce_scatter x1, waiting for transfers between devices, body(): lax.psum_scatter(partial_sum, 'row', scatter_dimension=0, tiled=True)  31.3 us
    all_gather x1, waiting for transfers between devices, body(): lax.all_gather(directions, 'col', axis=0, tiled=True)  17.8 us
  transfers between devices with their start and end apart: 5, of which 5 were waited for; matrix products, arithmetic and copies ran while one was open for 15% of the time, Pallas kernels for 0%

commit v1 on v0

--- a/solution.py
+++ b/solution.py
@@ -17,10 +17,18 @@
 
 
 def body(design, arc_filter, arc_of_row, terr_stored, block_order, directions):
+
+    def slabs_supply_all(panel):
+        built = lax.axis_size("col")
+        long_array = jnp.stack(built * [panel])
+        inter = lax.all_to_all(long_array, "col", split_axis=0, concat_axis=0)
+        block_out = jnp.concatenate(inter, axis=0)
+        return block_out
+
     whitened = whiten(design, arc_filter, arc_of_row)
     own_width = whitened.shape[0]
     rows_block, terr_rows = (
-        lax.all_gather(whitened, "col", axis=0, tiled=True),
+        slabs_supply_all(whitened),
         lax.all_gather(terr_stored, "col", axis=0, tiled=True),
     )
     cols_block = lax.all_gather(whitened, "row", axis=0, tiled=True)

time: 641 us -> 677 us (1.056)
  waiting for transfers between devices: 494 us -> 516 us
  local copies, waits for them, and re-layouts: 5.85 us -> 13.3 us
  starting transfers between devices: 0.19 us -> 7.59 us
    all_gather x1, waiting for transfers between devices: 32.6 us -> 420 us  [body(): lax.all_gather(terr_stored, 'col', axis=0, tiled=True)]
    all_gather x1 -> x0, waiting for transfers between devices: 364 us -> none  [body(): lax.all_gather(whitened, 'col', axis=0, tiled=True)]
    all_to_all x0 -> x1, starting transfers between devices: none -> 7.44 us  [slabs_supply_all(): inter = lax.all_to_all(long_array, 'col', split_axis=0, concat_axis=0)]
    another operation x0 -> x1, local copies, waits for them, and re-layouts: none -> 7.19 us  [slabs_supply_all(): long_array = jnp.stack(built * [panel])]
  transfers between devices with their start and end apart: 5 -> 5, of which waited for: 5 -> 4; matrix products, arithmetic and copies ran while one was open for 15% -> 12% of each run, Pallas kernels for 0% -> 0%
where the time goes in v1:
time: 677 us
  waiting for transfers between devices  516 us (76%)
  matrix products  107 us (16%)
  other arithmetic  19.3 us (3%)
  between operations  13.9 us (2%)
  local copies, waits for them, and re-layouts  13.3 us (2%)
  starting transfers between devices  7.59 us (1%)
    all_gather x1, waiting for transfers between devices, body(): lax.all_gather(terr_stored, 'col', axis=0, tiled=True)  420 us
    dot_general x1, matrix products, body(): lax.dot_general(cols_block, rows_block, (((1,), (1,)), ((), ())), preferr...  53.3 us
    all_gather x1, waiting for transfers between devices, body(): cols_block = lax.all_gather(whitened, 'row', axis=0, tiled=True)  44.3 us
    dot_general x1, matrix products, body(): jnp.dot(normal_tile, lax.all_gather(directions, 'col', axis=0, tiled=True...  38.9 us
    reduce_scatter x1, waiting for transfers between devices, body(): lax.psum_scatter(partial_sum, 'row', scatter_dimension=0, tiled=True)  31.3 us
    all_gather x1, waiting for transfers between devices, body(): lax.all_gather(directions, 'col', axis=0, tiled=True)  18 us
  transfers between devices with their start and end apart: 5, of which 4 were waited for; matrix products, arithmetic and copies ran while one was open for 12% of the time, Pallas kernels for 0%

profile of v1, /device:TPU:0, one launch (start us, length us, event | category | flops | bytes accessed | tf_op | source)
XLA Modules:
  0.0 676.8 jit_solution(2122635762939635738)
XLA Ops:
  7.2 10.8 %fusion.7 = bf16[576,2048]{1,0:T(8,128)(2,1)S(1)} fusion(bf16[576,2048]{1,0:T(8,128)(2,1)} %param.6, bf16[2048,2048]{1,0:T(8,128)(2,1)} %param.7, s32[2048]{0:T(1024)} %param.8), kind=kOutput, calls=%fused_computation.10 | convolution fusion | flops 4852154368 | bytes 13115392 | tf_op jit(solution)/shard_map/dot_general | solution.py:13
  18.0 7.2 %stack.2 = bf16[8,576,2048]{2,1,0:T(8,128)(2,1)} broadcast(bf16[576,2048]{1,0:T(8,128)(2,1)S(1)} %fusion.7), dimensions={1,2} | broadcast | bytes 21233664 | tf_op jit(solution)/shard_map/stack | solution.py:23
  25.2 7.4 %all-to-all-start = ((bf16[8,576,2048]{2,1,0:T(8,128)(2,1)}), bf16[8,576,2048]{2,1,0:T(8,128)(2,1)}, u32[]{:S(2)}, u32[]{:S(2)}) async-start(bf16[8,576,2048]{2,1,0:T(8,128)(2,1)} %stack.2), calls=%async_computation | async-start | bytes 37748736 | tf_op jit(solution)/shard_map/all_to_all | solution.py:24
  32.6 0.0 all-gather.6.cloned.1.call-start
  32.6 0.7 all-gather.6.cloned.1.call-update
  33.3 0.0 all-gather.4.cloned.1.call-start
  33.4 0.7 all-gather.4.cloned.1.call-update
  34.1 0.0 all-gather.8.cloned.1.call-start
  34.1 0.7 all-gather.8.cloned.1.call-update
  34.8 0.0 reduce-scatter.2.cloned.1.call-start
  35.0 0.1 fusion.15
  35.1 420.3 %all-gather.6.cloned.1.call-done = bf16[4608,128]{1,0:T(8,128)(2,1)} async-done(((bf16[576,128]{1,0:T(8,128)(2,1)}), bf16[4608,128]{1,0:T(8,128)(2,1)}) %all-gather.6.cloned.1.call-update) | async-done | bytes 1179664 | tf_op jit(solution)/shard_map/all_gather | solution.py:32
  455.5 1.9 copy.12
  457.4 1.8 broadcast_select_fusion
  459.2 3.7 copy.14
  462.9 3.8 fusion.11
  466.7 0.5 copy.15
  467.2 7.0 %broadcast_multiply_fusion = f32[576,36,128]{2,1,0:T(8,128)} fusion(f32[576,128]{1,0:T(8,128)S(1)} %constant_dynamic-slice_fusion, f32[576,36]{1,0:T(8,128)S(1)} %fusion.15), kind=kLoop, calls=%fused_computation.8 | loop fusion | flops 2654208 | bytes 10994688 | tf_op jit(solution)/shard_map/mul | solution.py:57
  474.2 44.3 %all-gather.4.cloned.1.call-done = bf16[2304,2048]{1,0:T(8,128)(2,1)} async-done(((bf16[576,2048]{1,0:T(8,128)(2,1)}), bf16[2304,2048]{1,0:T(8,128)(2,1)}) %all-gather.4.cloned.1.call-update) | async-done | bytes 9437200 | tf_op jit(solution)/shard_map/all_gather | solution.py:34
  518.5 53.3 %fusion.24 = f32[2304,4608]{1,0:T(8,128)} fusion(bf16[2304,2048]{1,0:T(8,128)(2,1)} %all-gather.4.cloned.1.call-done, bf16[4608,2048]{1,0:T(8,128)(2,1)} %bitcast.1), kind=kOutput, calls=%fused_computation.39 | convolution fusion | flops 43486543872 | bytes 70778880 | tf_op jit(solution)/shard_map/dot_general | solution.py:35
  571.8 10.3 %fusion.2 = f32[2304,4608]{1,0:T(8,128)} fusion(f32[2304,4608]{1,0:T(8,128)} %fusion.24, s32[]{:T(128)S(6)} %select_n.29, f32[72,8,36,128]{3,2,1,0:T(8,128)S(1)} %bitcast.28), kind=kLoop, calls=%fused_computation.4 | loop fusion | flops 2654208 | bytes 31850500 | tf_op jit(solution)/shard_map/dynamic_update_slice | solution.py:59
  582.0 18.0 %all-gather.8.cloned.1.call-done = f32[4608,256]{1,0:T(8,128)} async-done(((f32[576,256]{1,0:T(8,128)}), f32[4608,256]{1,0:T(8,128)}) %all-gather.8.cloned.1.call-update) | async-done | bytes 4718608 | tf_op jit(solution)/shard_map/all_gather | solution.py:65
  600.0 38.9 %fusion.25 = f32[2304,256]{1,0:T(8,128)} fusion(f32[2304,4608]{1,0:T(8,128)} %fusion.2, f32[4608,256]{1,0:T(8,128)} %all-gather.8.cloned.1.call-done), kind=kOutput, calls=%fused_computation.40 | convolution fusion | flops 32614907904 | bytes 49545216 | tf_op jit(solution)/shard_map/dot_general | solution.py:63
  638.9 31.3 %reduce-scatter.2.cloned.1.call-done = f32[576,256]{1,0:T(8,128)} async-done(((f32[2304,256]{1,0:T(8,128)}), f32[576,256]{1,0:T(8,128)}) %reduce-scatter.2.cloned.1.call-update) | async-done | bytes 589840 | tf_op jit(solution)/shard_map/reduce_scatter | solution.py:69
  (14 shorter events, 0.1 us)
Async XLA Ops:
  18.0 7.2 %copy-start.1 = (bf16[576,2048]{1,0:T(8,128)(2,1)}, bf16[576,2048]{1,0:T(8,128)(2,1)S(1)}, u32[]{:S(2)}) copy-start(bf16[576,2048]{1,0:T(8,128)(2,1)S(1)} %fusion.7) | copy-start | bytes 7077892
  25.2 9.8 %copy-start.2 = (s32[36]{0:T(128)S(1)}, s32[36]{0:T(128)}, u32[]{:S(2)}) copy-start(s32[36]{0:T(128)} %param.10) | copy-start | bytes 436
  25.2 493.3 %all-to-all-start = ((bf16[8,576,2048]{2,1,0:T(8,128)(2,1)}), bf16[8,576,2048]{2,1,0:T(8,128)(2,1)}, u32[]{:S(2)}, u32[]{:S(2)}) async-start(bf16[8,576,2048]{2,1,0:T(8,128)(2,1)} %stack.2), calls=%async_computation | async-start | bytes 37748736 | tf_op jit(solution)/shard_map/all_to_all | solution.py:24
  32.6 422.9 %all-gather.6.cloned.1.call-start = ((), (), s32[]{:S(2)}) async-start(), calls=%async_computation.3 | async-start | bytes 1327104 | tf_op jit(solution)/shard_map/all_gather | solution.py:32
  33.3 485.1 %all-gather.4.cloned.1.call-start = ((), (), s32[]{:S(2)}) async-start(), calls=%async_computation.2 | async-start | bytes 11796480 | tf_op jit(solution)/shard_map/all_gather | solution.py:34
  34.1 565.9 %all-gather.8.cloned.1.call-start = ((), (), s32[]{:S(2)}) async-start(), calls=%async_computation.4 | async-start | bytes 5308416 | tf_op jit(solution)/shard_map/all_gather | solution.py:65
  34.8 635.4 %reduce-scatter.2.cloned.1.call-start = ((), (), s32[]{:S(2)}) async-start(), calls=%async_computation.5 | async-start | bytes 2949120 | tf_op jit(solution)/shard_map/reduce_scatter | solution.py:69
  518.5 53.3 %copy-start = (f32[576,36,128]{2,1,0:T(8,128)S(1)}, f32[576,36,128]{2,1,0:T(8,128)}, u32[]{:S(2)}) copy-start(f32[576,36,128]{2,1,0:T(8,128)} %broadcast_multiply_fusion) | copy-start | bytes 31850500
Sparse Core Ops, SparseCore 0:
  35.6 419.8 all-gather.5
  457.0 61.4 all-gather.3
  520.7 79.3 all-gather.7
  639.1 31.1 reduce-scatter.1
